TPU v7x, 32 devices: a whole 2x2x4 slice. The times are simulated.
32 devices in a mesh: groups: 2 (over x), loop: 16 (over z, y, core).
Axes of the slice: x: 2, y: 2, z: 4, core: 2. Of those that a mesh axis runs over, the one named last changes fastest.
Arguments:
- queries: bfloat16 [16384, 2048], P(('groups', 'loop')), parts along dimension 0, may hold values from -16 to 16, as said below
- key_rows: bfloat16 [16384, 2048], P(('groups', 'loop')), parts along dimension 0, may hold values from -12 to 12, as said below
- values: bfloat16 [16384, 2048], P(('groups', 'loop')), parts along dimension 0, may hold values from -24 to 24
Outputs:
- attended: bfloat16 [16384, 2048], P(('groups', 'loop')), parts along dimension 0
- profile: float32 [4096], P('groups'), parts along dimension 0
There are 2 independent parts, one for each index of `groups`. A program takes and returns all parts, laid end to end along the dimension named above; each array names one. Nothing has to cross between parts.
Inputs may be any that keep to these rules, and one draw needn't show every extreme that they name: Real-valued queries. `key_rows`: Real-valued keys of order one.
All inputs are finite; a program needn't handle non-finite values.
Results may differ from a plain program's by a relative error of at most 0.0049.
Values may be sent and summed in bfloat16 or wider, within the bound.
A program may use at most 128 MiB of HBM per device.

v0:
```python
import math
import jax
import jax.numpy as jnp
from jax import lax
from jax.sharding import PartitionSpec as P

HEADS = 16
HEAD_DIM = 128
WINDOW = 2048


def passed_along(value, axis, steps):
    count = lax.axis_size(axis)
    pairs = [(source, (source + steps) % count) for source in range(count)]
    return lax.ppermute(value, axis, pairs)


def attend(query_block, key_ext, value_ext):
    row_count = query_block.shape[0]
    ext_count = key_ext.shape[0]
    scale = HEAD_DIM ** (-0.5)
    query_pos = lax.broadcasted_iota(jnp.int32, (row_count, ext_count), 0)
    key_pos = lax.broadcasted_iota(jnp.int32, (row_count, ext_count), 1)
    allowed = (key_pos > query_pos) & (key_pos <= query_pos + WINDOW)

    def one_head(head_index, output_buf):
        column = head_index * HEAD_DIM
        q_head = lax.dynamic_slice_in_dim(query_block, column, HEAD_DIM, 1)
        k_head = lax.dynamic_slice_in_dim(key_ext, column, HEAD_DIM, 1)
        v_head = lax.dynamic_slice_in_dim(value_ext, column, HEAD_DIM, 1)
        scores = (
            lax.dot_general(
                q_head, k_head, (((1,), (1,)), ((), ())), preferred_element_type=jnp.float32
            )
            * scale
        )
        scores = jnp.where(allowed, scores, jnp.float32(-1e30))
        top = jnp.max(scores, axis=1, keepdims=True)
        expo = jnp.exp(scores - top)
        weights = (expo / jnp.sum(expo, axis=1, keepdims=True)).astype(jnp.bfloat16)
        head_out = jnp.dot(weights, v_head, preferred_element_type=jnp.float32).astype(jnp.bfloat16)
        return lax.dynamic_update_slice_in_dim(output_buf, head_out, column, 1)

    return lax.fori_loop(0, HEADS, one_head, jnp.zeros(query_block.shape, jnp.bfloat16))


def body(queries, key_rows, values):
    row_count = queries.shape[0]
    reach_count = WINDOW // row_count
    near_keys, near_values = passed_along((key_rows, values), "loop", 1)
    for level in range(reach_count.bit_length() - 1):
        far_keys, far_values = passed_along((near_keys, near_values), "loop", 1 << level)
        near_keys = jnp.concatenate([far_keys, near_keys], axis=0)
        near_values = jnp.concatenate([far_values, near_values], axis=0)
    key_ext = jnp.concatenate([near_keys, key_rows], axis=0)
    value_ext = jnp.concatenate([near_values, values], axis=0)
    attended = attend(queries, key_ext, value_ext)
    local_sum = jnp.sum(attended.astype(jnp.float32), axis=0)
    total = lax.psum(local_sum, "loop")
    profile = total / math.sqrt(row_count * lax.axis_size("loop"))
    return (attended, profile)


def solution(mesh):
    return jax.shard_map(
        body,
        mesh=mesh,
        in_specs=(
            P(("groups", "loop"), None),
            P(("groups", "loop"), None),
            P(("groups", "loop"), None),
        ),
        out_specs=(P(("groups", "loop"), None), P("groups")),
        check_vma=False,
    )
```

profile of v0, /device:TPU:0, one launch (start us, length us, event | category | flops | bytes accessed | tf_op | source)
XLA Modules:
  0.0 416.9 jit_solution(2512011049518232460)
XLA Ops:
  1.1 2.6 collective-permute-start
  3.8 26.3 %collective-permute-done.3 = bf16[512,2048]{1,0:T(8,128)(2,1)S(1)} collective-permute-done((bf16[512,2048]{1,0:T(8,128)(2,1)}, bf16[512,2048]{1,0:T(8,128)(2,1)S(1)}, u32[]{:S(2)}, u32[]{:S(2)}) %collective-permute-start.3) | collective-permute-done | bytes 2097184 | tf_op jit(solution)/shard_map/ppermute | solution.py:15
  30.1 22.5 %collective-permute-done = bf16[512,2048]{1,0:T(8,128)(2,1)S(1)} collective-permute-done((bf16[512,2048]{1,0:T(8,128)(2,1)}, bf16[512,2048]{1,0:T(8,128)(2,1)S(1)}, u32[]{:S(2)}, u32[]{:S(2)}) %collective-permute-start) | collective-permute-done | bytes 2097184 | tf_op jit(solution)/shard_map/ppermute | solution.py:15
  52.5 22.5 %collective-permute-done.4 = bf16[512,2048]{1,0:T(8,128)(2,1)S(1)} collective-permute-done((bf16[512,2048]{1,0:T(8,128)(2,1)S(1)}, bf16[512,2048]{1,0:T(8,128)(2,1)S(1)}, u32[]{:S(2)}, u32[]{:S(2)}) %collective-permute-start.4) | collective-permute-done | bytes 2097184 | tf_op jit(solution)/shard_map/ppermute | solution.py:15
  75.0 2.6 pad_maximum_fusion.3
  77.6 33.3 %collective-permute-done.1 = bf16[512,2048]{1,0:T(8,128)(2,1)S(1)} collective-permute-done((bf16[512,2048]{1,0:T(8,128)(2,1)S(1)}, bf16[512,2048]{1,0:T(8,128)(2,1)S(1)}, u32[]{:S(2)}, u32[]{:S(2)}) %collective-permute-start.1) | collective-permute-done | bytes 2097184 | tf_op jit(solution)/shard_map/ppermute | solution.py:15
  110.8 1.3 copy-done.1
  112.2 2.6 pad_maximum_fusion.2
  114.8 1.2 collective-permute-start.2
  116.0 58.1 %collective-permute-done.5 = bf16[1024,2048]{1,0:T(8,128)(2,1)} collective-permute-done((bf16[1024,2048]{1,0:T(8,128)(2,1)}, bf16[1024,2048]{1,0:T(8,128)(2,1)}, u32[]{:S(2)}, u32[]{:S(2)}) %collective-permute-start.5) | collective-permute-done | bytes 4194336 | tf_op jit(solution)/shard_map/ppermute | solution.py:15
  174.1 10.2 %pad_maximum_fusion.1 = bf16[2560,2048]{1,0:T(8,128)(2,1)} fusion(bf16[512,2048]{1,0:T(8,128)(2,1)} %param.7, bf16[512,2048]{1,0:T(8,128)(2,1)} %copy-done, bf16[512,2048]{1,0:T(8,128)(2,1)} %copy-done.3, bf16[1024,2048]{1,0:T(8,128)(2,1)} %collective-permute-done.5), kind=kLoop, calls=%fused_computation.17 | loop fusion | flops 41943040 | bytes 20971520 | tf_op jit(solution)/shard_map/concatenate | solution.py:56
  184.3 79.7 %collective-permute-done.2 = bf16[1024,2048]{1,0:T(8,128)(2,1)} collective-permute-done((bf16[1024,2048]{1,0:T(8,128)(2,1)}, bf16[1024,2048]{1,0:T(8,128)(2,1)}, u32[]{:S(2)}, u32[]{:S(2)}) %collective-permute-start.2) | collective-permute-done | bytes 4194336 | tf_op jit(solution)/shard_map/ppermute | solution.py:15
  264.0 13.6 %pad_maximum_fusion = bf16[2560,2048]{1,0:T(8,128)(2,1)} fusion(bf16[512,2048]{1,0:T(8,128)(2,1)S(1)} %copy-done.5, bf16[512,2048]{1,0:T(8,128)(2,1)S(1)} %collective-permute-done, bf16[512,2048]{1,0:T(8,128)(2,1)S(1)} %copy-done.2, bf16[1024,2048]{1,0:T(8,128)(2,1)} %collective-permute-done.2), kind=kLoop, calls=%fused_computation.16 | loop fusion | flops 41943040 | bytes 20971520 | tf_op jit(solution)/shard_map/concatenate | solution.py:55
  277.8 93.0 %while.14 = (s32[]{:T(128)}, bf16[512,2048]{1,0:T(8,128)(2,1)S(1)}, bf16[512,2048]{1,0:T(8,128)(2,1)}, bf16[2560,2048]{1,0:T(8,128)(2,1)}, bf16[2560,2048]{1,0:T...) while((s32[]{:T(128)}, bf16[512,2048]{1,0:T(8,128)(2,1)S(1)}, ...), condition=%wide.region_3.4_spmd.clone, body=%wide.region_0.3_spmd.clone.sunk | while | flops 685571072 | bytes 17315988 | solution.py:44
  277.8 2.8 fusion.18
  280.6 0.8 fusion.19
  281.5 2.1 fusion.20
  283.6 2.8 fusion.18
  287.3 2.1 fusion.20
  289.4 2.8 fusion.18
  293.1 2.1 fusion.20
  295.2 2.8 fusion.18
  298.9 2.1 fusion.20
  301.0 2.8 fusion.18
  304.7 2.1 fusion.20
  306.9 2.8 fusion.18
  310.5 2.1 fusion.20
  312.7 2.8 fusion.18
  316.3 2.1 fusion.20
  318.5 2.8 fusion.18
  322.1 2.1 fusion.20
  324.3 2.8 fusion.18
  328.0 2.1 fusion.20
  330.1 2.8 fusion.18
  333.8 2.1 fusion.20
  335.9 2.8 fusion.18
  339.6 2.1 fusion.20
  341.7 2.8 fusion.18
  345.4 2.1 fusion.20
  347.5 2.8 fusion.18
  351.2 2.1 fusion.20
  353.4 2.8 fusion.18
  357.0 2.1 fusion.20
  359.2 2.8 fusion.18
  362.8 2.1 fusion.20
  365.0 2.8 fusion.18
  368.6 2.1 fusion.20
  371.2 45.1 %psum.7 = f32[2048]{0:T(1024)S(1)} all-reduce(f32[2048]{0:T(1024)S(1)} %convert_reduce_fusion), channel_id=1, replica_groups=mesh['groups'=2,'loop'=16] {'loop'}, use_global_device_ids=true, to_apply=%region_5.6 | all-reduce | flops 2048 | bytes 16384 | tf_op jit(solution)/shard_map/psum | solution.py:59
  (34 shorter events, 14.4 us)
Async XLA Ops:
  0.6 29.4 %collective-permute-start.3 = (bf16[512,2048]{1,0:T(8,128)(2,1)}, bf16[512,2048]{1,0:T(8,128)(2,1)S(1)}, u32[]{:S(2)}, u32[]{:S(2)}) collective-permute-start(bf16[512,2048]{1,0:T(8,128)(2,1)} %param.7), channel_id=1, source_target_pairs={{0,1},{1,2},{2,3},{3,4},{4,5},{5,6},{6,7},{7,8},{8,9},{9,10},{10,1... | collective-permute-start | bytes 6291464 | tf_op jit(solution)/shard_map/ppermute | solution.py:15
  1.1 51.4 %collective-permute-start = (bf16[512,2048]{1,0:T(8,128)(2,1)}, bf16[512,2048]{1,0:T(8,128)(2,1)S(1)}, u32[]{:S(2)}, u32[]{:S(2)}) collective-permute-start(bf16[512,2048]{1,0:T(8,128)(2,1)} %param.6), channel_id=1, source_target_pairs={{0,1},{1,2},{2,3},{3,4},{4,5},{5,6},{6,7},{7,8},{8,9},{9,10},{10,1... | collective-permute-start | bytes 6291464 | tf_op jit(solution)/shard_map/ppermute | solution.py:15
  30.1 84.7 %copy-start = (bf16[512,2048]{1,0:T(8,128)(2,1)}, bf16[512,2048]{1,0:T(8,128)(2,1)S(1)}, u32[]{:S(2)}) copy-start(bf16[512,2048]{1,0:T(8,128)(2,1)S(1)} %collective-permute-done.3) | copy-start | bytes 6291460
  30.1 44.9 %collective-permute-start.4 = (bf16[512,2048]{1,0:T(8,128)(2,1)S(1)}, bf16[512,2048]{1,0:T(8,128)(2,1)S(1)}, u32[]{:S(2)}, u32[]{:S(2)}) collective-permute-start(bf16[512,2048]{1,0:T(8,128)(2,1)S(1)} %collective-permute-done.3), channel_id=1, source_target_pairs={{0,1},{1,2},{2,3},{3,4},{4,5},{5,6},{6,7},{7,8},{8,9},{9,10},{10,1... | collective-permute-start | bytes 6291464 | tf_op jit(solution)/shard_map/ppermute | solution.py:15
  52.5 58.3 %collective-permute-start.1 = (bf16[512,2048]{1,0:T(8,128)(2,1)S(1)}, bf16[512,2048]{1,0:T(8,128)(2,1)S(1)}, u32[]{:S(2)}, u32[]{:S(2)}) collective-permute-start(bf16[512,2048]{1,0:T(8,128)(2,1)S(1)} %collective-permute-done), channel_id=1, source_target_pairs={{0,1},{1,2},{2,3},{3,4},{4,5},{5,6},{6,7},{7,8},{8,9},{9,10},{10,1... | collective-permute-start | bytes 6291464 | tf_op jit(solution)/shard_map/ppermute | solution.py:15
  75.0 39.8 %copy-start.3 = (bf16[512,2048]{1,0:T(8,128)(2,1)}, bf16[512,2048]{1,0:T(8,128)(2,1)S(1)}, u32[]{:S(2)}) copy-start(bf16[512,2048]{1,0:T(8,128)(2,1)S(1)} %collective-permute-done.4) | copy-start | bytes 6291460
  77.6 96.5 %collective-permute-start.5 = (bf16[1024,2048]{1,0:T(8,128)(2,1)}, bf16[1024,2048]{1,0:T(8,128)(2,1)}, u32[]{:S(2)}, u32[]{:S(2)}) collective-permute-start(bf16[1024,2048]{1,0:T(8,128)(2,1)} %pad_maximum_fusion.3), channel_id=1, source_target_pairs={{0,2},{1,3},{2,4},{3,5},{4,6},{5,7},{6,8},{7,9},{8,10},{9,11},{10,... | collective-permute-start | bytes 12582920 | tf_op jit(solution)/shard_map/ppermute | solution.py:15
  110.8 1.3 copy-start.1
  114.8 149.2 %collective-permute-start.2 = (bf16[1024,2048]{1,0:T(8,128)(2,1)}, bf16[1024,2048]{1,0:T(8,128)(2,1)}, u32[]{:S(2)}, u32[]{:S(2)}) collective-permute-start(bf16[1024,2048]{1,0:T(8,128)(2,1)} %pad_maximum_fusion.2), channel_id=1, source_target_pairs={{0,2},{1,3},{2,4},{3,5},{4,6},{5,7},{6,8},{7,9},{8,10},{9,11},{10,... | collective-permute-start | bytes 12582920 | tf_op jit(solution)/shard_map/ppermute | solution.py:15
  116.0 148.0 %copy-start.2 = (bf16[512,2048]{1,0:T(8,128)(2,1)S(1)}, bf16[512,2048]{1,0:T(8,128)(2,1)}, u32[]{:S(2)}) copy-start(bf16[512,2048]{1,0:T(8,128)(2,1)} %copy-done.1) | copy-start | bytes 6291460
  116.0 148.0 %copy-start.5 = (bf16[512,2048]{1,0:T(8,128)(2,1)S(1)}, bf16[512,2048]{1,0:T(8,128)(2,1)}, u32[]{:S(2)}) copy-start(bf16[512,2048]{1,0:T(8,128)(2,1)} %param.6) | copy-start | bytes 6291460
  370.8 46.1 %copy-start.4 = (bf16[512,2048]{1,0:T(8,128)(2,1)}, bf16[512,2048]{1,0:T(8,128)(2,1)S(1)}, u32[]{:S(2)}) copy-start(bf16[512,2048]{1,0:T(8,128)(2,1)S(1)} %get-tuple-element.109) | copy-start | bytes 6291460
where the time goes:
time: 418 us; the launch traced here: 417 us
  waiting for transfers between devices  242 us (58%)
  matrix products  79.1 us (19%)
  blocking collectives  45.1 us (11%)
  other arithmetic  43.5 us (10%)
  starting transfers between devices  4.36 us (1%)
    ppermute x6, waiting for transfers between devices, passed_along(): return lax.ppermute(value, axis, pairs)  242 us
    psum x1, blocking collectives, body(): total = lax.psum(local_sum, 'loop')  45.1 us
    dot_general x16, matrix products, one_head(): lax.dot_general(q_head, k_head, (((1,), (1,)), ((), ())), preferred_eleme...  45 us
    dot_general x16, matrix products, one_head(): jnp.dot(weights, v_head, preferred_element_type=jnp.float32)  34.1 us
    concatenate x1, other arithmetic, body(): key_ext = jnp.concatenate([near_keys, key_rows], axis=0)  13.6 us
    reduce_sum x16, other arithmetic, one_head(): weights = (expo / jnp.sum(expo, axis=1, keepdims=True)).astype(jnp.bfloat16)  13.5 us
    concatenate x1, other arithmetic, body(): value_ext = jnp.concatenate([near_values, values], axis=0)  10.2 us
  transfers between devices with their start and end apart: 6, of which 6 were waited for; matrix products, arithmetic and copies ran while one was open for 4% of the time, Pallas kernels for 0%

commit v1 on v0

--- a/solution.py
+++ b/solution.py
@@ -56,7 +56,7 @@
     value_ext = jnp.concatenate([near_values, values], axis=0)
     attended = attend(queries, key_ext, value_ext)
     local_sum = jnp.sum(attended.astype(jnp.float32), axis=0)
-    total = lax.psum(local_sum, "loop")
+    total = jnp.sum(lax.all_gather(local_sum, "loop"), axis=0)
     profile = total / math.sqrt(row_count * lax.axis_size("loop"))
     return (attended, profile)
 

time: 418 us -> 404 us (0.967)
  blocking collectives: 45.1 us -> 30.6 us
    psum x1 -> x0, blocking collectives: 45.1 us -> none  [body(): total = lax.psum(local_sum, 'loop')]
    all_gather x0 -> x1, blocking collectives: none -> 30.6 us  [body(): total = jnp.sum(lax.all_gather(local_sum, 'loop'), axis=0)]
where the time goes in v1:
time: 404 us; the launch traced here: 402 us
  waiting for transfers between devices  242 us (60%)
  matrix products  79.1 us (20%)
  other arithmetic  43.5 us (11%)
  blocking collectives  30.6 us (8%)
  starting transfers between devices  4.36 us (1%)
    ppermute x6, waiting for transfers between devices, passed_along(): return lax.ppermute(value, axis, pairs)  242 us
    dot_general x16, matrix products, one_head(): lax.dot_general(q_head, k_head, (((1,), (1,)), ((), ())), preferred_eleme...  45 us
    dot_general x16, matrix products, one_head(): jnp.dot(weights, v_head, preferred_element_type=jnp.float32)  34.1 us
    all_gather x1, blocking collectives, body(): total = jnp.sum(lax.all_gather(local_sum, 'loop'), axis=0)  30.6 us
    concatenate x1, other arithmetic, body(): key_ext = jnp.concatenate([near_keys, key_rows], axis=0)  13.6 us
    reduce_sum x16, other arithmetic, one_head(): weights = (expo / jnp.sum(expo, axis=1, keepdims=True)).astype(jnp.bfloat16)  13.5 us
    concatenate x1, other arithmetic, body(): value_ext = jnp.concatenate([near_values, values], axis=0)  10.2 us
  transfers between devices with their start and end apart: 6, of which 6 were waited for; matrix products, arithmetic and copies ran while one was open for 4% of the time, Pallas kernels for 0%

profile of v1, /device:TPU:0, one launch (start us, length us, event | category | flops | bytes accessed | tf_op | source)
XLA Modules:
  0.0 402.5 jit_solution(17978572449359556612)
XLA Ops:
  1.1 2.6 collective-permute-start
  3.8 26.3 %collective-permute-done.3 = bf16[512,2048]{1,0:T(8,128)(2,1)S(1)} collective-permute-done((bf16[512,2048]{1,0:T(8,128)(2,1)}, bf16[512,2048]{1,0:T(8,128)(2,1)S(1)}, u32[]{:S(2)}, u32[]{:S(2)}) %collective-permute-start.3) | collective-permute-done | bytes 2097184 | tf_op jit(solution)/shard_map/ppermute | solution.py:15
  30.1 22.5 %collective-permute-done = bf16[512,2048]{1,0:T(8,128)(2,1)S(1)} collective-permute-done((bf16[512,2048]{1,0:T(8,128)(2,1)}, bf16[512,2048]{1,0:T(8,128)(2,1)S(1)}, u32[]{:S(2)}, u32[]{:S(2)}) %collective-permute-start) | collective-permute-done | bytes 2097184 | tf_op jit(solution)/shard_map/ppermute | solution.py:15
  52.5 22.5 %collective-permute-done.4 = bf16[512,2048]{1,0:T(8,128)(2,1)S(1)} collective-permute-done((bf16[512,2048]{1,0:T(8,128)(2,1)S(1)}, bf16[512,2048]{1,0:T(8,128)(2,1)S(1)}, u32[]{:S(2)}, u32[]{:S(2)}) %collective-permute-start.4) | collective-permute-done | bytes 2097184 | tf_op jit(solution)/shard_map/ppermute | solution.py:15
  75.0 2.6 pad_maximum_fusion.3
  77.6 33.3 %collective-permute-done.1 = bf16[512,2048]{1,0:T(8,128)(2,1)S(1)} collective-permute-done((bf16[512,2048]{1,0:T(8,128)(2,1)S(1)}, bf16[512,2048]{1,0:T(8,128)(2,1)S(1)}, u32[]{:S(2)}, u32[]{:S(2)}) %collective-permute-start.1) | collective-permute-done | bytes 2097184 | tf_op jit(solution)/shard_map/ppermute | solution.py:15
  110.8 1.3 copy-done.1
  112.2 2.6 pad_maximum_fusion.2
  114.8 1.2 collective-permute-start.2
  116.0 58.1 %collective-permute-done.5 = bf16[1024,2048]{1,0:T(8,128)(2,1)} collective-permute-done((bf16[1024,2048]{1,0:T(8,128)(2,1)}, bf16[1024,2048]{1,0:T(8,128)(2,1)}, u32[]{:S(2)}, u32[]{:S(2)}) %collective-permute-start.5) | collective-permute-done | bytes 4194336 | tf_op jit(solution)/shard_map/ppermute | solution.py:15
  174.1 10.2 %pad_maximum_fusion.1 = bf16[2560,2048]{1,0:T(8,128)(2,1)} fusion(bf16[512,2048]{1,0:T(8,128)(2,1)} %param.7, bf16[512,2048]{1,0:T(8,128)(2,1)} %copy-done, bf16[512,2048]{1,0:T(8,128)(2,1)} %copy-done.3, bf16[1024,2048]{1,0:T(8,128)(2,1)} %collective-permute-done.5), kind=kLoop, calls=%fused_computation.17 | loop fusion | flops 41943040 | bytes 20971520 | tf_op jit(solution)/shard_map/concatenate | solution.py:56
  184.3 79.7 %collective-permute-done.2 = bf16[1024,2048]{1,0:T(8,128)(2,1)} collective-permute-done((bf16[1024,2048]{1,0:T(8,128)(2,1)}, bf16[1024,2048]{1,0:T(8,128)(2,1)}, u32[]{:S(2)}, u32[]{:S(2)}) %collective-permute-start.2) | collective-permute-done | bytes 4194336 | tf_op jit(solution)/shard_map/ppermute | solution.py:15
  264.0 13.6 %pad_maximum_fusion = bf16[2560,2048]{1,0:T(8,128)(2,1)} fusion(bf16[512,2048]{1,0:T(8,128)(2,1)S(1)} %copy-done.5, bf16[512,2048]{1,0:T(8,128)(2,1)S(1)} %collective-permute-done, bf16[512,2048]{1,0:T(8,128)(2,1)S(1)} %copy-done.2, bf16[1024,2048]{1,0:T(8,128)(2,1)} %collective-permute-done.2), kind=kLoop, calls=%fused_computation.16 | loop fusion | flops 41943040 | bytes 20971520 | tf_op jit(solution)/shard_map/concatenate | solution.py:55
  277.8 93.0 %while.14 = (s32[]{:T(128)}, bf16[512,2048]{1,0:T(8,128)(2,1)S(1)}, bf16[512,2048]{1,0:T(8,128)(2,1)}, bf16[2560,2048]{1,0:T(8,128)(2,1)}, bf16[2560,2048]{1,0:T...) while((s32[]{:T(128)}, bf16[512,2048]{1,0:T(8,128)(2,1)S(1)}, ...), condition=%wide.region_3.4_spmd.clone, body=%wide.region_0.3_spmd.clone.sunk | while | flops 685571072 | bytes 17315988 | solution.py:44
  277.8 2.8 fusion.18
  280.6 0.8 fusion.19
  281.5 2.1 fusion.20
  283.6 2.8 fusion.18
  287.3 2.1 fusion.20
  289.4 2.8 fusion.18
  293.1 2.1 fusion.20
  295.2 2.8 fusion.18
  298.9 2.1 fusion.20
  301.0 2.8 fusion.18
  304.7 2.1 fusion.20
  306.9 2.8 fusion.18
  310.5 2.1 fusion.20
  312.7 2.8 fusion.18
  316.3 2.1 fusion.20
  318.5 2.8 fusion.18
  322.1 2.1 fusion.20
  324.3 2.8 fusion.18
  328.0 2.1 fusion.20
  330.1 2.8 fusion.18
  333.8 2.1 fusion.20
  335.9 2.8 fusion.18
  339.6 2.1 fusion.20
  341.7 2.8 fusion.18
  345.4 2.1 fusion.20
  347.5 2.8 fusion.18
  351.2 2.1 fusion.20
  353.4 2.8 fusion.18
  357.0 2.1 fusion.20
  359.2 2.8 fusion.18
  362.8 2.1 fusion.20
  365.0 2.8 fusion.18
  368.6 2.1 fusion.20
  371.2 30.6 %all-gather = f32[32768]{0:T(1024)S(1)} all-gather(f32[2048]{0:T(1024)S(1)} %convert_reduce_fusion), channel_id=2, replica_groups=mesh['groups'=2,'loop'=16] {'loop'}, dimensions={0}, use_global_device_ids=true | all-gather | bytes 139264 | tf_op jit(solution)/shard_map/all_gather | solution.py:59
  (36 shorter events, 14.5 us)
Async XLA Ops:
  0.6 29.4 %collective-permute-start.3 = (bf16[512,2048]{1,0:T(8,128)(2,1)}, bf16[512,2048]{1,0:T(8,128)(2,1)S(1)}, u32[]{:S(2)}, u32[]{:S(2)}) collective-permute-start(bf16[512,2048]{1,0:T(8,128)(2,1)} %param.7), channel_id=1, source_target_pairs={{0,1},{1,2},{2,3},{3,4},{4,5},{5,6},{6,7},{7,8},{8,9},{9,10},{10,1... | collective-permute-start | bytes 6291464 | tf_op jit(solution)/shard_map/ppermute | solution.py:15
  1.1 51.4 %collective-permute-start = (bf16[512,2048]{1,0:T(8,128)(2,1)}, bf16[512,2048]{1,0:T(8,128)(2,1)S(1)}, u32[]{:S(2)}, u32[]{:S(2)}) collective-permute-start(bf16[512,2048]{1,0:T(8,128)(2,1)} %param.6), channel_id=1, source_target_pairs={{0,1},{1,2},{2,3},{3,4},{4,5},{5,6},{6,7},{7,8},{8,9},{9,10},{10,1... | collective-permute-start | bytes 6291464 | tf_op jit(solution)/shard_map/ppermute | solution.py:15
  30.1 84.7 %copy-start = (bf16[512,2048]{1,0:T(8,128)(2,1)}, bf16[512,2048]{1,0:T(8,128)(2,1)S(1)}, u32[]{:S(2)}) copy-start(bf16[512,2048]{1,0:T(8,128)(2,1)S(1)} %collective-permute-done.3) | copy-start | bytes 6291460
  30.1 44.9 %collective-permute-start.4 = (bf16[512,2048]{1,0:T(8,128)(2,1)S(1)}, bf16[512,2048]{1,0:T(8,128)(2,1)S(1)}, u32[]{:S(2)}, u32[]{:S(2)}) collective-permute-start(bf16[512,2048]{1,0:T(8,128)(2,1)S(1)} %collective-permute-done.3), channel_id=1, source_target_pairs={{0,1},{1,2},{2,3},{3,4},{4,5},{5,6},{6,7},{7,8},{8,9},{9,10},{10,1... | collective-permute-start | bytes 6291464 | tf_op jit(solution)/shard_map/ppermute | solution.py:15
  52.5 58.3 %collective-permute-start.1 = (bf16[512,2048]{1,0:T(8,128)(2,1)S(1)}, bf16[512,2048]{1,0:T(8,128)(2,1)S(1)}, u32[]{:S(2)}, u32[]{:S(2)}) collective-permute-start(bf16[512,2048]{1,0:T(8,128)(2,1)S(1)} %collective-permute-done), channel_id=1, source_target_pairs={{0,1},{1,2},{2,3},{3,4},{4,5},{5,6},{6,7},{7,8},{8,9},{9,10},{10,1... | collective-permute-start | bytes 6291464 | tf_op jit(solution)/shard_map/ppermute | solution.py:15
  75.0 39.8 %copy-start.3 = (bf16[512,2048]{1,0:T(8,128)(2,1)}, bf16[512,2048]{1,0:T(8,128)(2,1)S(1)}, u32[]{:S(2)}) copy-start(bf16[512,2048]{1,0:T(8,128)(2,1)S(1)} %collective-permute-done.4) | copy-start | bytes 6291460
  77.6 96.5 %collective-permute-start.5 = (bf16[1024,2048]{1,0:T(8,128)(2,1)}, bf16[1024,2048]{1,0:T(8,128)(2,1)}, u32[]{:S(2)}, u32[]{:S(2)}) collective-permute-start(bf16[1024,2048]{1,0:T(8,128)(2,1)} %pad_maximum_fusion.3), channel_id=1, source_target_pairs={{0,2},{1,3},{2,4},{3,5},{4,6},{5,7},{6,8},{7,9},{8,10},{9,11},{10,... | collective-permute-start | bytes 12582920 | tf_op jit(solution)/shard_map/ppermute | solution.py:15
  110.8 1.3 copy-start.1
  114.8 149.2 %collective-permute-start.2 = (bf16[1024,2048]{1,0:T(8,128)(2,1)}, bf16[1024,2048]{1,0:T(8,128)(2,1)}, u32[]{:S(2)}, u32[]{:S(2)}) collective-permute-start(bf16[1024,2048]{1,0:T(8,128)(2,1)} %pad_maximum_fusion.2), channel_id=1, source_target_pairs={{0,2},{1,3},{2,4},{3,5},{4,6},{5,7},{6,8},{7,9},{8,10},{9,11},{10,... | collective-permute-start | bytes 12582920 | tf_op jit(solution)/shard_map/ppermute | solution.py:15
  116.0 148.0 %copy-start.2 = (bf16[512,2048]{1,0:T(8,128)(2,1)S(1)}, bf16[512,2048]{1,0:T(8,128)(2,1)}, u32[]{:S(2)}) copy-start(bf16[512,2048]{1,0:T(8,128)(2,1)} %copy-done.1) | copy-start | bytes 6291460
  116.0 148.0 %copy-start.5 = (bf16[512,2048]{1,0:T(8,128)(2,1)S(1)}, bf16[512,2048]{1,0:T(8,128)(2,1)}, u32[]{:S(2)}) copy-start(bf16[512,2048]{1,0:T(8,128)(2,1)} %param.6) | copy-start | bytes 6291460
  370.8 31.7 %copy-start.4 = (bf16[512,2048]{1,0:T(8,128)(2,1)}, bf16[512,2048]{1,0:T(8,128)(2,1)S(1)}, u32[]{:S(2)}) copy-start(bf16[512,2048]{1,0:T(8,128)(2,1)S(1)} %get-tuple-element.109) | copy-start | bytes 6291460
